TPU v7x, 32 devices: a whole 2x2x4 slice. The times are simulated.
32 devices in a mesh: dp: 8 (over y, x, core), tensor: 4 (over z).
Axes of the slice: x: 2, y: 2, z: 4, core: 2. Of those that a mesh axis runs over, the one named last changes fastest.
Arguments:
- hidden_in: float32 [8192, 1536], P(('dp', 'tensor')), may hold values from -6 to 6
- cotangent: float32 [8192, 1536], P(('dp', 'tensor')), may hold values from -6 to 6
- seq_lengths: int32 [8, 4], P('dp'), may hold values from 1 to 512, 1024 in all within a row
- query_weight: bfloat16 [1536, 1536], P('dp', 'tensor'), may hold values from -0.15625 to 0.15625
- key_weight: bfloat16 [1536, 768], P('dp', 'tensor'), may hold values from -0.15625 to 0.15625
- value_weight: bfloat16 [1536, 768], P('dp', 'tensor'), may hold values from -0.15625 to 0.15625
- output_weight: bfloat16 [1536, 1536], P('tensor', 'dp'), may hold values from -1.25 to 1.25
- w_gate: bfloat16 [1536, 4096], P('dp', 'tensor'), may hold values from -0.15625 to 0.15625
- w_up: bfloat16 [1536, 4096], P('dp', 'tensor'), may hold values from -0.15625 to 0.15625
- w_down: bfloat16 [4096, 1536], P('tensor', 'dp'), may hold values from -0.09375 to 0.09375
- gain_attn: bfloat16 [1536], P('dp'), may hold values from 0.099609375 to 1.8984375
- gain_mlp: bfloat16 [1536], P('dp'), may hold values from 0.099609375 to 1.8984375
Outputs:
- block_out: float32 [8192, 1536], P(('dp', 'tensor'))
- grad_input: float32 [8192, 1536], P(('dp', 'tensor'))
- grad_query: float32 [1536, 1536], P('dp', 'tensor')
- grad_key: float32 [1536, 768], P('dp', 'tensor')
- grad_value: float32 [1536, 768], P('dp', 'tensor')
- grad_output: float32 [1536, 1536], P('tensor', 'dp')
- grad_gate: float32 [1536, 4096], P('dp', 'tensor')
- grad_upproj: float32 [1536, 4096], P('dp', 'tensor')
- grad_down: float32 [4096, 1536], P('tensor', 'dp')
- grad_attnorm: float32 [1536], P('dp')
- grad_mlpnorm: float32 [1536], P('dp')
Inputs may be any that keep to these rules, and one draw needn't show every extreme that they name: `seq_lengths`: each row's lengths sum to 1024, and the longest of each row is exactly 512.
All inputs are finite; a program needn't handle non-finite values.
Results may differ from a plain program's by a relative error of at most 0.02.
Values may be sent and summed in bfloat16 or wider, within the bound.
No kernel may reach another device: no remote copies, remote signals or barrier semaphores. Data moves between devices by JAX's collectives and lax.ppermute only.
A program may use at most 128 MiB of HBM per device.

v0:
```python
import math
import jax
import jax.numpy as jnp
from jax import lax
from jax.sharding import PartitionSpec as P

QUERY_HEADS = 16
KEY_VALUE_HEADS = 8
HEAD_SIZE = 96
EPS = 1e-05
ROPE_BASE = 100000.0


def product(formula, left_side, right_side):
    return jnp.einsum(formula, left_side, right_side, preferred_element_type=jnp.float32)


def matrix_multiply(left_side, right_side):
    return jnp.dot(left_side, right_side, preferred_element_type=jnp.float32)


def multiply_by_transpose(left_side, right_side):
    return lax.dot_general(
        left_side, right_side, (((1,), (1,)), ((), ())), preferred_element_type=jnp.float32
    )


def transposed_times(left_side, right_side):
    return lax.dot_general(
        left_side, right_side, (((0,), (0,)), ((), ())), preferred_element_type=jnp.float32
    )


def positions_of(lengths_row, length_all):
    seq_ends = jnp.cumsum(lengths_row)
    seq_starts = seq_ends - lengths_row
    token_index = jnp.arange(length_all, dtype=jnp.int32)
    segment = jnp.sum((token_index[:, None] >= seq_ends[None, :]).astype(jnp.int32), axis=1)
    chosen = segment[:, None] == jnp.arange(lengths_row.shape[0], dtype=jnp.int32)[None, :]
    offsets = jnp.sum(jnp.where(chosen, seq_starts[None, :], 0), axis=1)
    return (segment, token_index - offsets)


def rope_tables(position, head_width):
    half_width = head_width // 2
    frequency = jnp.exp(
        -(2.0 * jnp.arange(half_width, dtype=jnp.float32) / head_width)
        * jnp.log(jnp.float32(ROPE_BASE))
    )
    angles = position.astype(jnp.float32)[:, None] * frequency[None, :]
    return (jnp.cos(angles), jnp.sin(angles))


def rotate_fwd(value_tensor, cosine, sine):
    half_width = value_tensor.shape[-1] // 2
    front_half = value_tensor[..., :half_width]
    back_half = value_tensor[..., half_width:]
    return jnp.concatenate(
        [front_half * cosine - back_half * sine, back_half * cosine + front_half * sine], axis=-1
    )


def inverse_rotation(value_tensor, cosine, sine):
    half_width = value_tensor.shape[-1] // 2
    front_half = value_tensor[..., :half_width]
    back_half = value_tensor[..., half_width:]
    return jnp.concatenate(
        [front_half * cosine + back_half * sine, back_half * cosine - front_half * sine], axis=-1
    )


def norm_forward(value_tensor, gain_vector):
    inverse = lax.rsqrt(jnp.mean(value_tensor * value_tensor, axis=-1, keepdims=True) + EPS)
    unit_rows = value_tensor * inverse
    return (unit_rows, inverse, (unit_rows * gain_vector.astype(jnp.float32)).astype(jnp.bfloat16))


def norm_backward(grad_normed, unit_rows, inverse, gain_vector):
    scaled = grad_normed * gain_vector.astype(jnp.float32)
    grad_gain = jnp.sum(grad_normed * unit_rows, axis=0)
    grad_rows = inverse * (
        scaled - unit_rows * jnp.mean(scaled * unit_rows, axis=-1, keepdims=True)
    )
    return (grad_rows, grad_gain)


def block_scores(query_block, key_rows, segment_block, index_block, segment, factor):
    scores = product("qkgd,skd->kgqs", query_block, key_rows) * factor
    length_all = key_rows.shape[0]
    allowed = (segment_block[:, None] == segment[None, :]) & (
        jnp.arange(length_all, dtype=jnp.int32)[None, :] <= index_block[:, None]
    )
    return jnp.where(allowed[None, None], scores, -jnp.inf)


def attend(queries, key_rows, value_row_block, segment, block_rows):
    length_all, kv_heads, query_group_width, head_width = queries.shape
    blocks = length_all // block_rows
    factor = 1.0 / math.sqrt(head_width)
    token_index = jnp.arange(length_all, dtype=jnp.int32)

    def per_block(pieces):
        query_block, segment_block, index_block = pieces
        scores = block_scores(query_block, key_rows, segment_block, index_block, segment, factor)
        maximum = jnp.max(scores, axis=-1, keepdims=True)
        logsum = maximum + jnp.log(jnp.sum(jnp.exp(scores - maximum), axis=-1, keepdims=True))
        weights = jnp.exp(scores - logsum).astype(jnp.bfloat16)
        mixed = product("kgqs,skd->qkgd", weights, value_row_block).astype(jnp.bfloat16)
        return (mixed, logsum[..., 0])

    mixed, logsum = lax.map(
        per_block,
        (
            queries.reshape(blocks, block_rows, kv_heads, query_group_width, head_width),
            segment.reshape(blocks, block_rows),
            token_index.reshape(blocks, block_rows),
        ),
    )
    return (mixed.reshape(length_all, kv_heads, query_group_width, head_width), logsum)


def attend_back(
    queries, key_rows, value_row_block, mixed, mixed_gradient, logsum, segment, block_rows
):
    length_all, kv_heads, query_group_width, head_width = queries.shape
    blocks = length_all // block_rows
    factor = 1.0 / math.sqrt(head_width)
    token_index = jnp.arange(length_all, dtype=jnp.int32)

    def per_block(carry, pieces):
        grad_keys, grad_values = carry
        query_block, mixed_block, grad_block, logsum_block, segment_block, index_block = pieces
        scores = block_scores(query_block, key_rows, segment_block, index_block, segment, factor)
        probability = jnp.exp(scores - logsum_block[..., None])
        grad_values = grad_values + product(
            "kgqs,qkgd->skd", probability.astype(jnp.bfloat16), grad_block
        )
        grad_probs = product("qkgd,skd->kgqs", grad_block, value_row_block)
        row_delta = jnp.sum(
            grad_block.astype(jnp.float32) * mixed_block.astype(jnp.float32), axis=-1
        )
        row_delta = jnp.transpose(row_delta, (1, 2, 0))[..., None]
        grad_scores = (probability * (grad_probs - row_delta) * factor).astype(jnp.bfloat16)
        grad_query = product("kgqs,skd->qkgd", grad_scores, key_rows)
        grad_keys = grad_keys + product("kgqs,qkgd->skd", grad_scores, query_block)
        return ((grad_keys, grad_values), grad_query)

    empty_grad = jnp.zeros((length_all, kv_heads, head_width), jnp.float32)
    shape_blocks = (blocks, block_rows, kv_heads, query_group_width, head_width)
    (grad_keys, grad_values), grad_query = lax.scan(
        per_block,
        (empty_grad, empty_grad),
        (
            queries.reshape(shape_blocks),
            mixed.reshape(shape_blocks),
            mixed_gradient.reshape(shape_blocks),
            logsum,
            segment.reshape(blocks, block_rows),
            token_index.reshape(blocks, block_rows),
        ),
    )
    return (
        grad_query.reshape(length_all, kv_heads, query_group_width, head_width),
        grad_keys,
        grad_values,
    )


def local(
    hidden_in,
    cotangent,
    seq_lengths,
    query_weight,
    key_weight,
    value_weight,
    output_weight,
    w_gate,
    w_up,
    w_down,
    gain_attn,
    gain_mlp,
):
    query_group_width = QUERY_HEADS // KEY_VALUE_HEADS
    gathered = (
        lax.all_gather(query_weight, "dp", axis=0, tiled=True),
        lax.all_gather(key_weight, "dp", axis=0, tiled=True),
        lax.all_gather(value_weight, "dp", axis=0, tiled=True),
        lax.all_gather(output_weight, "dp", axis=1, tiled=True),
        lax.all_gather(w_gate, "dp", axis=0, tiled=True),
        lax.all_gather(w_up, "dp", axis=0, tiled=True),
        lax.all_gather(w_down, "dp", axis=1, tiled=True),
        lax.all_gather(gain_attn, "dp", axis=0, tiled=True),
        lax.all_gather(gain_mlp, "dp", axis=0, tiled=True),
    )
    (
        query_full,
        key_full,
        value_full,
        output_full,
        gate_full,
        up_full,
        down_full,
        gain_one,
        gain_two,
    ) = gathered
    kv_local = key_full.shape[1] // HEAD_SIZE
    unit_one, inverse_one, normed_rows_one = norm_forward(hidden_in, gain_one)
    first_normalized = lax.all_gather(normed_rows_one, "tensor", axis=0, tiled=True)
    tok_rows = first_normalized.shape[0]
    block_rows = min(512, tok_rows)
    segment, position = positions_of(seq_lengths[0], tok_rows)
    cosine, sine = rope_tables(position, HEAD_SIZE)
    cos_heads, sin_heads = (cosine[:, None, None, :], sine[:, None, None, :])
    cosine_key_table, sine_key_table = (cosine[:, None, :], sine[:, None, :])
    unrotated_queries = matrix_multiply(first_normalized, query_full).reshape(
        tok_rows, kv_local, query_group_width, HEAD_SIZE
    )
    unrotated_keys = matrix_multiply(first_normalized, key_full).reshape(
        tok_rows, kv_local, HEAD_SIZE
    )
    value_row_block = (
        matrix_multiply(first_normalized, value_full)
        .astype(jnp.bfloat16)
        .reshape(tok_rows, kv_local, HEAD_SIZE)
    )
    query_rot = rotate_fwd(unrotated_queries, cos_heads, sin_heads).astype(jnp.bfloat16)
    key_rot = rotate_fwd(unrotated_keys, cosine_key_table, sine_key_table).astype(jnp.bfloat16)
    query_rot, key_rot, value_row_block = (query_rot, key_rot, value_row_block)
    mixed, logsum = attend(query_rot, key_rot, value_row_block, segment, block_rows)
    mixed_flat = mixed.reshape(tok_rows, -1)
    residual = hidden_in + lax.psum_scatter(
        matrix_multiply(mixed_flat, output_full), "tensor", scatter_dimension=0, tiled=True
    )
    unit_two, inverse_two, normed_rows_two = norm_forward(residual, gain_two)
    normed_two = lax.all_gather(normed_rows_two, "tensor", axis=0, tiled=True)
    gate_rows = matrix_multiply(normed_two, gate_full)
    up_rows = matrix_multiply(normed_two, up_full)
    sigmoid_gate = jax.nn.sigmoid(gate_rows)
    silu_gate = gate_rows * sigmoid_gate
    project_hidden_act = (silu_gate * up_rows).astype(jnp.bfloat16)
    gate_rows, up_rows, sigmoid_gate, silu_gate, hidden_act = (
        gate_rows,
        up_rows,
        sigmoid_gate,
        silu_gate,
        project_hidden_act,
    )
    block_out = residual + lax.psum_scatter(
        matrix_multiply(hidden_act, down_full).astype(jnp.bfloat16),
        "tensor",
        scatter_dimension=0,
        tiled=True,
    ).astype(jnp.float32)
    gathered = (
        lax.all_gather(query_weight, "dp", axis=0, tiled=True),
        lax.all_gather(key_weight, "dp", axis=0, tiled=True),
        lax.all_gather(value_weight, "dp", axis=0, tiled=True),
        lax.all_gather(output_weight, "dp", axis=1, tiled=True),
        lax.all_gather(w_gate, "dp", axis=0, tiled=True),
        lax.all_gather(w_up, "dp", axis=0, tiled=True),
        lax.all_gather(w_down, "dp", axis=1, tiled=True),
        lax.all_gather(gain_attn, "dp", axis=0, tiled=True),
        lax.all_gather(gain_mlp, "dp", axis=0, tiled=True),
    )
    (
        query_full,
        key_full,
        value_full,
        output_full,
        gate_full,
        up_full,
        down_full,
        gain_one,
        gain_two,
    ) = gathered
    cot_low = lax.all_gather(cotangent.astype(jnp.bfloat16), "tensor", axis=0, tiled=True)
    grad_act = multiply_by_transpose(cot_low, down_full)
    grad_down = transposed_times(hidden_act, cot_low)
    grad_gate_rows = (
        grad_act * up_rows * sigmoid_gate * (1.0 + gate_rows * (1.0 - sigmoid_gate))
    ).astype(jnp.bfloat16)
    grad_up_rows = (grad_act * silu_gate).astype(jnp.bfloat16)
    grad_gate = transposed_times(normed_two, grad_gate_rows)
    grad_upproj = transposed_times(normed_two, grad_up_rows)
    grad_normed_two = lax.psum_scatter(
        (
            multiply_by_transpose(grad_gate_rows, gate_full)
            + multiply_by_transpose(grad_up_rows, up_full)
        ).astype(jnp.bfloat16),
        "tensor",
        scatter_dimension=0,
        tiled=True,
    ).astype(jnp.float32)
    grad_middle, grad_gain_two = norm_backward(grad_normed_two, unit_two, inverse_two, gain_two)
    grad_resid = cotangent + grad_middle
    narrow_gradient = lax.all_gather(grad_resid.astype(jnp.bfloat16), "tensor", axis=0, tiled=True)
    grad_output = transposed_times(mixed_flat, narrow_gradient)
    mixed_gradient = (
        multiply_by_transpose(narrow_gradient, output_full)
        .astype(jnp.bfloat16)
        .reshape(tok_rows, kv_local, query_group_width, HEAD_SIZE)
    )
    grad_qrot, rotated_key_gradient, gradient_values_list = attend_back(
        query_rot, key_rot, value_row_block, mixed, mixed_gradient, logsum, segment, block_rows
    )
    grad_q = (
        inverse_rotation(grad_qrot, cos_heads, sin_heads).astype(jnp.bfloat16).reshape(tok_rows, -1)
    )
    key_gradient = (
        inverse_rotation(rotated_key_gradient, cosine_key_table, sine_key_table)
        .astype(jnp.bfloat16)
        .reshape(tok_rows, -1)
    )
    value_gradient = gradient_values_list.astype(jnp.bfloat16).reshape(tok_rows, -1)
    grad_query = transposed_times(first_normalized, grad_q)
    grad_key = transposed_times(first_normalized, key_gradient)
    grad_value = transposed_times(first_normalized, value_gradient)
    grad_normed_one = lax.psum_scatter(
        (
            multiply_by_transpose(grad_q, query_full)
            + multiply_by_transpose(key_gradient, key_full)
            + multiply_by_transpose(value_gradient, value_full)
        ).astype(jnp.bfloat16),
        "tensor",
        scatter_dimension=0,
        tiled=True,
    ).astype(jnp.float32)
    grad_first, grad_gain_one = norm_backward(grad_normed_one, unit_one, inverse_one, gain_one)
    grad_input = grad_resid + grad_first
    summed = (
        lax.psum_scatter(
            grad_query.astype(jnp.bfloat16), "dp", scatter_dimension=0, tiled=True
        ).astype(jnp.float32),
        lax.psum_scatter(
            grad_key.astype(jnp.bfloat16), "dp", scatter_dimension=0, tiled=True
        ).astype(jnp.float32),
        lax.psum_scatter(
            grad_value.astype(jnp.bfloat16), "dp", scatter_dimension=0, tiled=True
        ).astype(jnp.float32),
        lax.psum_scatter(
            grad_output.astype(jnp.bfloat16), "dp", scatter_dimension=1, tiled=True
        ).astype(jnp.float32),
        lax.psum_scatter(
            grad_gate.astype(jnp.bfloat16), "dp", scatter_dimension=0, tiled=True
        ).astype(jnp.float32),
        lax.psum_scatter(
            grad_upproj.astype(jnp.bfloat16), "dp", scatter_dimension=0, tiled=True
        ).astype(jnp.float32),
        lax.psum_scatter(
            grad_down.astype(jnp.bfloat16), "dp", scatter_dimension=1, tiled=True
        ).astype(jnp.float32),
        lax.psum_scatter(
            grad_gain_one.astype(jnp.bfloat16), "dp", scatter_dimension=0, tiled=True
        ).astype(jnp.float32),
        lax.psum_scatter(
            grad_gain_two.astype(jnp.bfloat16), "dp", scatter_dimension=0, tiled=True
        ).astype(jnp.float32),
    )
    output_grad = summed[3]
    gain_totals = lax.psum((summed[7], summed[8]), "tensor")
    return (
        block_out,
        grad_input,
        summed[0],
        summed[1],
        summed[2],
        output_grad,
        summed[4],
        summed[5],
        summed[6],
        gain_totals[0],
        gain_totals[1],
    )


def solution(mesh):
    in_specs = (
        P(("dp", "tensor"), None),
        P(("dp", "tensor"), None),
        P("dp", None),
        P("dp", "tensor"),
        P("dp", "tensor"),
        P("dp", "tensor"),
        P("tensor", "dp"),
        P("dp", "tensor"),
        P("dp", "tensor"),
        P("tensor", "dp"),
        P("dp"),
        P("dp"),
    )
    out_specs = (
        P(("dp", "tensor"), None),
        P(("dp", "tensor"), None),
        P("dp", "tensor"),
        P("dp", "tensor"),
        P("dp", "tensor"),
        P("tensor", "dp"),
        P("dp", "tensor"),
        P("dp", "tensor"),
        P("tensor", "dp"),
        P("dp"),
        P("dp"),
    )
    return jax.shard_map(local, mesh=mesh, in_specs=in_specs, out_specs=out_specs, check_vma=False)
```

profile of v0, /device:TPU:0, one launch (start us, length us, event | category | flops | bytes accessed | tf_op | source)
XLA Modules:
  0.0 1093.3 jit_solution(17131380025793593165)
XLA Ops:
  12.6 16.0 %all-reduce.6 = (bf16[1536]{0:T(1024)(128)(2,1)S(1)}, bf16[1536]{0:T(1024)(128)(2,1)}) all-reduce(bf16[1536]{0:T(1024)(128)(2,1)S(1)} %dynamic-update-slice, bf16[1536]{0:T(1024)(128)(2,1)S(1)} %dynamic-update-slice.1), channel_id=1, replica_groups=mesh['dp'=8,'tensor'=4] {'dp'}, use_global_device_ids=true, to_apply=%add | all-reduce | flops 3072 | bytes 12288
  33.8 10.5 all_gather.51
  44.3 11.2 %all_gather.52 = bf16[1536,192]{1,0:T(8,128)(2,1)} all-gather(bf16[192,192]{1,0:T(8,128)(2,1)S(1)} %copy-done.27), channel_id=1, replica_groups=mesh['dp'=8,'tensor'=4] {'dp'}, dimensions={0}, use_global_device_ids=true | all-gather | bytes 663552 | tf_op jit(solution)/shard_map/all_gather | solution.py:187
  56.3 37.9 %all-gather.10.cloned.1.call-done = bf16[1024,1536]{1,0:T(8,128)(2,1)} async-done(((bf16[256,1536]{1,0:T(8,128)(2,1)}), bf16[1024,1536]{1,0:T(8,128)(2,1)}) %all-gather.10.cloned.1.call-update) | async-done | bytes 3145744 | tf_op jit(solution)/shard_map/all_gather | solution.py:208
  98.4 20.2 %all-gather.12.cloned.1.call-done = bf16[1536,384]{1,0:T(8,128)(2,1)} async-done(((bf16[192,384]{1,0:T(8,128)(2,1)}), bf16[1536,384]{1,0:T(8,128)(2,1)}) %all-gather.12.cloned.1.call-update) | async-done | bytes 1179664 | tf_op jit(solution)/shard_map/all_gather | solution.py:185
  130.9 22.1 %while.27 = (s32[]{:T(128)}, bf16[2,512,2,2,96]{1,4,3,2,0:T(8,128)(2,1)}, f32[2,2,2,512]{3,2,1,0:T(2,128)}, s32[2,512]{1,0:T(2,128)}, s32[1024]{0:T(1024)S(1)}, ...) while((s32[]{:T(128)}, ...), condition=%wide.region_7.8_spmd, body=%wide.region_4.7_spmd.sunk | while | flops 830142464 | bytes 28917884 | solution.py:111
  161.9 110.3 %reduce-scatter.12.cloned.1.call-done = f32[256,1536]{1,0:T(8,128)} async-done(((f32[1024,1536]{1,0:T(8,128)}), f32[256,1536]{1,0:T(8,128)}) %reduce-scatter.12.cloned.1.call-update) | async-done | bytes 1572880 | tf_op jit(solution)/shard_map/reduce_scatter | solution.py:231
  279.2 27.5 %all-gather.20.cloned.1.call-done = bf16[1536,1024]{1,0:T(8,128)(2,1)} async-done(((bf16[192,1024]{1,0:T(8,128)(2,1)}), bf16[1536,1024]{1,0:T(8,128)(2,1)}) %all-gather.20.cloned.1.call-update) | async-done | bytes 3145744 | tf_op jit(solution)/shard_map/all_gather | solution.py:190
  306.6 65.5 %all-gather.16.cloned.1.call-done = bf16[1024,1536]{1,0:T(8,128)(2,1)} async-done(((bf16[256,1536]{1,0:T(8,128)(2,1)}), bf16[1024,1536]{1,0:T(8,128)(2,1)}) %all-gather.16.cloned.1.call-update) | async-done | bytes 3145744 | tf_op jit(solution)/shard_map/all_gather | solution.py:235
  372.1 8.3 fusion.80
  380.4 24.5 %all-gather.18.cloned.1.call-done = bf16[1536,1024]{1,0:T(8,128)(2,1)} async-done(((bf16[192,1024]{1,0:T(8,128)(2,1)}), bf16[1536,1024]{1,0:T(8,128)(2,1)}) %all-gather.18.cloned.1.call-update) | async-done | bytes 3145744 | tf_op jit(solution)/shard_map/all_gather | solution.py:189
  404.9 8.2 fusion.79
  413.1 57.4 %all-gather.24.cloned.1.call-done = bf16[1024,1536]{1,0:T(8,128)(2,1)} async-done(((bf16[256,1536]{1,0:T(8,128)(2,1)}), bf16[1024,1536]{1,0:T(8,128)(2,1)}) %all-gather.24.cloned.1.call-update) | async-done | bytes 3145744 | tf_op jit(solution)/shard_map/all_gather | solution.py:276
  470.5 32.7 %all-gather.22.cloned.1.call-done = bf16[1024,1536]{0,1:T(8,128)(2,1)} async-done(((bf16[1024,192]{0,1:T(8,128)(2,1)}), bf16[1024,1536]{0,1:T(8,128)(2,1)}) %all-gather.22.cloned.1.call-update) | async-done | bytes 3145744 | tf_op jit(solution)/shard_map/all_gather | solution.py:191
  503.2 11.6 %multiply_convert_fusion = (bf16[1024,1024]{1,0:T(8,128)(2,1)S(1)}, bf16[1024,1024]{1,0:T(8,128)(2,1)S(1)}, bf16[1024,1024]{1,0:T(8,128)(2,1)}) fusion(f32[1024,1024]{1,0:T(8,128)} %fusion.79, f32[1024,1024]{1,0:T(8,128)} %fusion.80, bf16[1024,1536]{1,0:T(8,128)(2,1)} %all-gather.24.cloned.1.call-done, bf16[1024,1536]{0,1:T(8,128)(2,1)} %all-gather.22.cloned.1.call-done), kind=kOutput, calls=%fused_computation.68 | convolution fusion | flops 3236954112 | bytes 20971520 | tf_op jit(solution)/shard_map/dot_general | solution.py:23
  523.5 60.5 %reduce-scatter.16.cloned.1.call-done = bf16[256,1536]{1,0:T(8,128)(2,1)} async-done(((bf16[1024,1536]{1,0:T(8,128)(2,1)}), bf16[256,1536]{1,0:T(8,128)(2,1)}) %reduce-scatter.16.cloned.1.call-update) | async-done | bytes 786448 | tf_op jit(solution)/shard_map/reduce_scatter | solution.py:285
  597.1 8.0 convolution_convert_fusion.1
  605.2 7.7 convolution_convert_fusion.2
  613.0 39.9 %all-gather.26.cloned.1.call-done = bf16[1024,1536]{1,0:T(8,128)(2,1)} async-done(((bf16[256,1536]{1,0:T(8,128)(2,1)}), bf16[1024,1536]{1,0:T(8,128)(2,1)}) %all-gather.26.cloned.1.call-update) | async-done | bytes 3145744 | tf_op jit(solution)/shard_map/all_gather | solution.py:296
  664.5 68.3 %while.28 = (s32[]{:T(128)}, f32[1024,2,96]{0,2,1:T(8,128)}, f32[1024,2,96]{0,2,1:T(8,128)}, f32[2,512,2,2,96]{1,0,4,3,2:T(2,128)}, bf16[2,512,2,2,96]{1,4,3,2,0...) while((s32[]{:T(128)}, f32[1024,2,96]{0,2,1:T(8,128)}, ...), condition=%wide.region_15.16_spmd.clone, body=%wide.region_13.15_spmd.clone.sunk | while | flops 2039478272 | bytes 50004156 | solution.py:150
  682.9 15.0 %dynamic_update_slice.20 = f32[2,512,2,2,96]{1,0,4,3,2:T(2,128)} dynamic-update-slice(f32[2,512,2,2,96]{1,0,4,3,2:T(2,128)} %get-tuple-element.535, f32[1,512,2,2,96]{1,0,4,3,2:T(1,128)S(1)} %copy.60, s32[]{:T(128)S(6)} %copy.79, s32[]{:T(128)} %constant.62.clone.1..sunk, s32[]{:T(128)} %constant.62.clone.1..sunk, s32[]{:T(128)} %constant.62.clone.1..sunk, s32[]{:T(128)} %constant.62.clone.1..sunk) | dynamic-update-slice | bytes 1572868 | tf_op jit(solution)/shard_map/while/body/jit(dynamic_update_index_in_dim)/dynamic_update_slice | solution.py:150
  717.8 15.0 %dynamic_update_slice.20 = f32[2,512,2,2,96]{1,0,4,3,2:T(2,128)} dynamic-update-slice(f32[2,512,2,2,96]{1,0,4,3,2:T(2,128)} %get-tuple-element.535, f32[1,512,2,2,96]{1,0,4,3,2:T(1,128)S(1)} %copy.60, s32[]{:T(128)S(6)} %copy.79, s32[]{:T(128)} %constant.62.clone.1..sunk, s32[]{:T(128)} %constant.62.clone.1..sunk, s32[]{:T(128)} %constant.62.clone.1..sunk, s32[]{:T(128)} %constant.62.clone.1..sunk) | dynamic-update-slice | bytes 1572868 | tf_op jit(solution)/shard_map/while/body/jit(dynamic_update_index_in_dim)/dynamic_update_slice | solution.py:150
  764.1 8.0 convolution_convert_fusion.3
  776.9 22.8 %reduce-scatter.28.cloned.1.call-done = bf16[192,1024]{1,0:T(8,128)(2,1)} async-done(((bf16[1536,1024]{1,0:T(8,128)(2,1)}), bf16[192,1024]{1,0:T(8,128)(2,1)}) %reduce-scatter.28.cloned.1.call-update) | async-done | bytes 393232 | tf_op jit(solution)/shard_map/reduce_scatter | solution.py:343
  801.6 36.0 %reduce-scatter.24.cloned.1.call-done = bf16[192,192]{1,0:T(8,128)(2,1)} async-done(((bf16[1536,192]{1,0:T(8,128)(2,1)}), bf16[192,192]{1,0:T(8,128)(2,1)}) %reduce-scatter.24.cloned.1.call-update) | async-done | bytes 73744 | tf_op jit(solution)/shard_map/reduce_scatter | solution.py:337
  839.2 36.4 %reduce-scatter.22.cloned.1.call-done = bf16[192,192]{1,0:T(8,128)(2,1)} async-done(((bf16[1536,192]{1,0:T(8,128)(2,1)}), bf16[192,192]{1,0:T(8,128)(2,1)}) %reduce-scatter.22.cloned.1.call-update) | async-done | bytes 73744 | tf_op jit(solution)/shard_map/reduce_scatter | solution.py:334
  877.2 38.8 %reduce-scatter.26.cloned.1.call-done = bf16[384,192]{0,1:T(8,128)(2,1)} async-done(((bf16[384,1536]{0,1:T(8,128)(2,1)}), bf16[384,192]{0,1:T(8,128)(2,1)}) %reduce-scatter.26.cloned.1.call-update) | async-done | bytes 147472 | tf_op jit(solution)/shard_map/reduce_scatter | solution.py:340
  917.6 38.7 %reduce-scatter.20.cloned.1.call-done = bf16[192,384]{1,0:T(8,128)(2,1)} async-done(((bf16[1536,384]{1,0:T(8,128)(2,1)}), bf16[192,384]{1,0:T(8,128)(2,1)}) %reduce-scatter.20.cloned.1.call-update) | async-done | bytes 147472 | tf_op jit(solution)/shard_map/reduce_scatter | solution.py:331
  958.0 61.1 %reduce-scatter.18.cloned.1.call-done = bf16[256,1536]{1,0:T(8,128)(2,1)} async-done(((bf16[1024,1536]{1,0:T(8,128)(2,1)}), bf16[256,1536]{1,0:T(8,128)(2,1)}) %reduce-scatter.18.cloned.1.call-update) | async-done | bytes 786448 | tf_op jit(solution)/shard_map/reduce_scatter | solution.py:318
  1020.8 13.5 %all-reduce.5 = (bf16[1536]{0:T(1024)(128)(2,1)S(1)}, bf16[1536]{0:T(1024)(128)(2,1)S(1)}) all-reduce(bf16[1536]{0:T(1024)(128)(2,1)S(1)} %get-tuple-element.256, bf16[1536]{0:T(1024)(128)(2,1)S(1)} %copy-done.32), channel_id=13, replica_groups=mesh['dp'=8,'tensor'=4] {'dp'}, use_global_device_ids=true, to_apply=%region_26.27.clone | all-reduce | flops 3072 | bytes 12288
  1034.4 12.1 %all-reduce.4 = (f32[192]{0:T(256)}, f32[192]{0:T(256)}) all-reduce(f32[192]{0:T(256)S(1)} %get-tuple-element.336, f32[192]{0:T(256)S(1)} %get-tuple-element.335), channel_id=1, replica_groups=mesh['dp'=8,'tensor'=4] {'tensor'}, use_global_device_ids=true, to_apply=%region_27.28 | all-reduce | flops 384 | bytes 3072 | tf_op jit(solution)/shard_map/psum | solution.py:360
  1046.5 35.3 %reduce-scatter.14.cloned.1.call-done = bf16[256,1536]{1,0:T(8,128)(2,1)} async-done(((bf16[1024,1536]{1,0:T(8,128)(2,1)}), bf16[256,1536]{1,0:T(8,128)(2,1)}) %reduce-scatter.14.cloned.1.call-update) | async-done | bytes 786448 | tf_op jit(solution)/shard_map/reduce_scatter | solution.py:248
  (231 shorter events, 186.0 us)
Async XLA Ops:
  7.2 87.0 %all-gather.10.cloned.1.call-start = ((), (), s32[]{:S(2)}) async-start(), calls=%async_computation.11 | async-start | bytes 3932160 | tf_op jit(solution)/shard_map/all_gather | solution.py:208
  31.2 87.4 %all-gather.12.cloned.1.call-start = ((), (), s32[]{:S(2)}) async-start(), calls=%async_computation.12 | async-start | bytes 1327104 | tf_op jit(solution)/shard_map/all_gather | solution.py:185
  31.9 123.2 %all-gather.14.cloned.1.call-start = ((), (), s32[]{:S(2)}) async-start(), calls=%async_computation.13 | async-start | bytes 1327104 | tf_op jit(solution)/shard_map/all_gather | solution.py:188
  32.7 239.5 %reduce-scatter.12.cloned.1.call-start = ((), (), s32[]{:S(2)}) async-start(), calls=%async_computation.14 | async-start | bytes 7864320 | tf_op jit(solution)/shard_map/reduce_scatter | solution.py:231
  56.3 65.1 %copy-start.10 = (f32[1024,48]{0,1:T(8,128)}, f32[1024,48]{0,1:T(8,128)S(1)}, u32[]{:S(2)}) copy-start(f32[1024,48]{0,1:T(8,128)S(1)} %get-tuple-element.331) | copy-start | bytes 589828
  56.3 65.1 %copy-start.12 = (f32[1024,48]{0,1:T(8,128)}, f32[1024,48]{0,1:T(8,128)S(1)}, u32[]{:S(2)}) copy-start(f32[1024,48]{0,1:T(8,128)S(1)} %get-tuple-element.332) | copy-start | bytes 589828
  161.2 111.0 %copy-start = (f32[256,1536]{1,0:T(8,128)S(1)}, f32[256,1536]{1,0:T(8,128)}, u32[]{:S(2)}) copy-start(f32[256,1536]{1,0:T(8,128)} %param.16) | copy-start | bytes 4718596
  161.2 145.4 %all-gather.20.cloned.1.call-start = ((), (), s32[]{:S(2)}) async-start(), calls=%async_computation.17 | async-start | bytes 3538944 | tf_op jit(solution)/shard_map/all_gather | solution.py:190
  161.8 210.3 %all-gather.16.cloned.1.call-start = ((), (), s32[]{:S(2)}) async-start(), calls=%async_computation.15 | async-start | bytes 3932160 | tf_op jit(solution)/shard_map/all_gather | solution.py:235
  161.9 115.0 %copy-start.4 = (f32[256,1536]{1,0:T(8,128)S(1)}, f32[256,1536]{1,0:T(8,128)}, u32[]{:S(2)}) copy-start(f32[256,1536]{1,0:T(8,128)} %param.17) | copy-start | bytes 4718596
  276.1 128.8 %all-gather.18.cloned.1.call-start = ((), (), s32[]{:S(2)}) async-start(), calls=%async_computation.16 | async-start | bytes 3538944 | tf_op jit(solution)/shard_map/all_gather | solution.py:189
  276.8 193.6 %all-gather.24.cloned.1.call-start = ((), (), s32[]{:S(2)}) async-start(), calls=%async_computation.20 | async-start | bytes 3932160 | tf_op jit(solution)/shard_map/all_gather | solution.py:276
  277.9 225.3 %all-gather.22.cloned.1.call-start = ((), (), s32[]{:S(2)}) async-start(), calls=%async_computation.18 | async-start | bytes 3538944 | tf_op jit(solution)/shard_map/all_gather | solution.py:191
  278.6 305.4 %reduce-scatter.16.cloned.1.call-start = ((), (), s32[]{:S(2)}) async-start(), calls=%async_computation.21 | async-start | bytes 3932160 | tf_op jit(solution)/shard_map/reduce_scatter | solution.py:285
  523.4 60.6 %copy-start.3 = (f32[256,1536]{1,0:T(8,128)S(1)}, f32[256,1536]{1,0:T(8,128)}, u32[]{:S(2)}) copy-start(f32[256,1536]{1,0:T(8,128)} %copy-done.2) | copy-start | bytes 4718596
  523.4 129.4 %all-gather.26.cloned.1.call-start = ((), (), s32[]{:S(2)}) async-start(), calls=%async_computation.22 | async-start | bytes 3932160 | tf_op jit(solution)/shard_map/all_gather | solution.py:296
  589.4 183.5 %reduce-scatter.32.cloned.1.call-start = ((), (), s32[]{:S(2)}) async-start(), calls=%async_computation.30 | async-start | bytes 3538944 | tf_op jit(solution)/shard_map/reduce_scatter | solution.py:349
  597.1 177.8 %reduce-scatter.30.cloned.1.call-start = ((), (), s32[]{:S(2)}) async-start(), calls=%async_computation.29 | async-start | bytes 3538944 | tf_op jit(solution)/shard_map/reduce_scatter | solution.py:346
  605.1 194.5 %reduce-scatter.28.cloned.1.call-start = ((), (), s32[]{:S(2)}) async-start(), calls=%async_computation.28 | async-start | bytes 3538944 | tf_op jit(solution)/shard_map/reduce_scatter | solution.py:343
  612.9 40.0 %copy-start.21 = (bf16[384,1536]{0,1:T(8,128)(2,1)S(1)}, bf16[384,1536]{0,1:T(8,128)(2,1)}, u32[]{:S(2)}) copy-start(bf16[384,1536]{0,1:T(8,128)(2,1)} %all-gather.14.cloned.1.call-done) | copy-start | bytes 3538948
  612.9 224.7 %reduce-scatter.24.cloned.1.call-start = ((), (), s32[]{:S(2)}) async-start(), calls=%async_computation.26 | async-start | bytes 884736 | tf_op jit(solution)/shard_map/reduce_scatter | solution.py:337
  738.8 136.9 %reduce-scatter.22.cloned.1.call-start = ((), (), s32[]{:S(2)}) async-start(), calls=%async_computation.25 | async-start | bytes 884736 | tf_op jit(solution)/shard_map/reduce_scatter | solution.py:334
  745.5 170.5 %reduce-scatter.26.cloned.1.call-start = ((), (), s32[]{:S(2)}) async-start(), calls=%async_computation.27 | async-start | bytes 1327104 | tf_op jit(solution)/shard_map/reduce_scatter | solution.py:340
  750.3 206.0 %reduce-scatter.20.cloned.1.call-start = ((), (), s32[]{:S(2)}) async-start(), calls=%async_computation.24 | async-start | bytes 1327104 | tf_op jit(solution)/shard_map/reduce_scatter | solution.py:331
  757.8 261.3 %reduce-scatter.18.cloned.1.call-start = ((), (), s32[]{:S(2)}) async-start(), calls=%async_computation.23 | async-start | bytes 3932160 | tf_op jit(solution)/shard_map/reduce_scatter | solution.py:318
  763.9 317.9 %reduce-scatter.14.cloned.1.call-start = ((), (), s32[]{:S(2)}) async-start(), calls=%async_computation.19 | async-start | bytes 3932160 | tf_op jit(solution)/shard_map/reduce_scatter | solution.py:248
  772.1 246.9 %copy-start.1 = (f32[256,1536]{1,0:T(8,128)S(1)}, f32[256,1536]{1,0:T(8,128)}, u32[]{:S(2)}) copy-start(f32[256,1536]{1,0:T(8,128)} %param.16) | copy-start | bytes 4718596
  772.1 246.9 %copy-start.25 = (f32[1536]{0:T(1024)S(1)}, f32[1536]{0:T(1024)}, u32[]{:S(2)}) copy-start(f32[1536]{0:T(1024)} %copy-done.24) | copy-start | bytes 18436
  772.1 246.9 %copy-start.31 = (f32[256]{0:T(256)S(1)}, f32[256]{0:T(256)}, u32[]{:S(2)}) copy-start(f32[256]{0:T(256)} %copy-done.30) | copy-start | bytes 3076
  774.9 245.9 %copy-start.32 = (bf16[1536]{0:T(1024)(128)(2,1)S(1)}, bf16[1536]{0:T(1024)(128)(2,1)}, u32[]{:S(2)}) copy-start(bf16[1536]{0:T(1024)(128)(2,1)} %get-tuple-element.254) | copy-start | bytes 9220
  774.9 306.9 %copy-start.29 = (f32[256]{0:T(256)S(1)}, f32[256]{0:T(256)}, u32[]{:S(2)}) copy-start(f32[256]{0:T(256)} %copy-done.28) | copy-start | bytes 3076
  774.9 306.9 %copy-start.34 = (f32[256]{0:T(256)S(1)}, f32[256]{0:T(256)}, u32[]{:S(2)}) copy-start(f32[256]{0:T(256)} %copy-done.33) | copy-start | bytes 3076
  (29 other events, 233.1 us)
Sparse Core Ops, SparseCore 0:
  31.3 62.7 all-gather.9
  96.0 22.5 all-gather.11
  120.5 23.9 all-gather.13
  161.4 110.7 reduce-scatter.11
  273.9 32.6 all-gather.19
  308.6 63.4 all-gather.15
  374.0 30.8 all-gather.17
  407.0 63.4 all-gather.23
  472.4 30.8 all-gather.21
  523.6 60.3 reduce-scatter.15
  589.5 63.3 all-gather.25
  656.1 44.6 reduce-scatter.31
  704.2 46.0 reduce-scatter.29
  753.6 46.0 reduce-scatter.27
  802.7 34.9 reduce-scatter.23
  840.6 34.9 reduce-scatter.21
  879.3 36.6 reduce-scatter.25
  919.6 36.6 reduce-scatter.19
  958.6 60.3 reduce-scatter.17
  1021.2 60.5 reduce-scatter.13
where the time goes:
time: 1100 us; the launch traced here: 1090 us
  waiting for transfers between devices  749 us (68%)
  matrix products  152 us (14%)
  blocking collectives  63.4 us (6%)
  local copies, waits for them, and re-layouts  60.7 us (6%)
  other arithmetic  49.9 us (5%)
  between operations  16.5 us (2%)
    reduce_scatter x1, waiting for transfers between devices, local(): lax.psum_scatter(matrix_multiply(mixed_flat, output_full), 'tensor', scat...  110 us
    all_gather x1, waiting for transfers between devices, local(): normed_two = lax.all_gather(normed_rows_two, 'tensor', axis=0, tiled=True)  65.5 us
    reduce_scatter x1, waiting for transfers between devices, local(): lax.psum_scatter((multiply_by_transpose(grad_q, query_full) + multiply_by...  61.1 us
    reduce_scatter x1, waiting for transfers between devices, local(): lax.psum_scatter((multiply_by_transpose(grad_gate_rows, gate_full) + mult...  60.5 us
    all_gather x1, waiting for transfers between devices, local(): lax.all_gather(cotangent.astype(jnp.bfloat16), 'tensor', axis=0, tiled=True)  57.4 us
    dot_general x14, matrix products, product(): jnp.einsum(formula, left_side, right_side, preferred_element_type=jnp.flo...  43.7 us
    all_gather x1, waiting for transfers between devices, local(): lax.all_gather(grad_resid.astype(jnp.bfloat16), 'tensor', axis=0, tiled=T...  39.9 us
    dot_general x7, matrix products, transposed_times(): lax.dot_general(left_side, right_side, (((0,), (0,)), ((), ())), preferre...  39 us
  transfers between devices with their start and end apart: 20, of which 17 were waited for; matrix products, arithmetic and copies ran while one was open for 20% of the time, Pallas kernels for 0%

commit v1 on v0

--- a/solution.py
+++ b/solution.py
@@ -273,7 +273,23 @@
         gain_one,
         gain_two,
     ) = gathered
-    cot_low = lax.all_gather(cotangent.astype(jnp.bfloat16), "tensor", axis=0, tiled=True)
+    array = cotangent.astype(jnp.bfloat16)
+    size, index, rows = (lax.axis_size("tensor"), lax.axis_index("tensor"), array.shape[0])
+    upward = [(i, (i + 1) % size) for i in range(size)]
+    downward = [(i, (i - 1) % size) for i in range(size)]
+    out = jnp.zeros((*array.shape[:0], size * rows, *array.shape[0 + 1 :]), array.dtype)
+    out = lax.dynamic_update_slice_in_dim(out, array, index * rows, axis=0)
+    from_left = from_right = array
+    half = size // 2
+    for lap in range(1, half + 1):
+        from_left = lax.ppermute(from_left, "tensor", upward)
+        out = lax.dynamic_update_slice_in_dim(out, from_left, (index - lap) % size * rows, axis=0)
+        if lap < size - half:
+            from_right = lax.ppermute(from_right, "tensor", downward)
+            out = lax.dynamic_update_slice_in_dim(
+                out, from_right, (index + lap) % size * rows, axis=0
+            )
+    cot_low = out
     grad_act = multiply_by_transpose(cot_low, down_full)
     grad_down = transposed_times(hidden_act, cot_low)
     grad_gate_rows = (

time: 1100 us -> 1050 us (0.955)
  waiting for transfers between devices: 749 us -> 676 us
  starting transfers between devices: 1.92 us -> 20.3 us
    all_gather x1 -> x0, waiting for transfers between devices: 57.4 us -> none  [local(): lax.all_gather(cotangent.astype(jnp.bfloat16), 'tensor', axis=0, tiled=True)]
    ppermute x0 -> x3, waiting for transfers between devices: none -> 48.9 us  [the longest x2 48.7 us: local(): from_left = lax.ppermute(from_left, 'tensor', upward)]
    all_gather x1, waiting for transfers between devices: 65.5 us -> 34.5 us  [local(): normed_two = lax.all_gather(normed_rows_two, 'tensor', axis=0, tiled=True)]
    all_gather x1, waiting for transfers between devices: 27.5 us -> 0.01 us  [local(): lax.all_gather(w_up, 'dp', axis=0, tiled=True)]
    ppermute x0 -> x3, starting transfers between devices: none -> 18.9 us  [the longest x2 16.5 us: local(): from_left = lax.ppermute(from_left, 'tensor', upward)]
  transfers between devices with their start and end apart: 20 -> 22, of which waited for: 17 -> 18; matrix products, arithmetic and copies ran while one was open for 20% -> 21% of each run, Pallas kernels for 0% -> 0%
where the time goes in v1:
time: 1050 us; the launch traced here: 1040 us
  waiting for transfers between devices  676 us (64%)
  matrix products  152 us (14%)
  local copies, waits for them, and re-layouts  66.4 us (6%)
  blocking collectives  63.4 us (6%)
  other arithmetic  50.3 us (5%)
  starting transfers between devices  20.3 us (2%)
  between operations  16.1 us (2%)
    reduce_scatter x1, waiting for transfers between devices, local(): lax.psum_scatter(matrix_multiply(mixed_flat, output_full), 'tensor', scat...  110 us
    reduce_scatter x1, waiting for transfers between devices, local(): lax.psum_scatter((multiply_by_transpose(grad_q, query_full) + multiply_by...  60.9 us
    reduce_scatter x1, waiting for transfers between devices, local(): lax.psum_scatter((multiply_by_transpose(grad_gate_rows, gate_full) + mult...  60.5 us
    ppermute x2, waiting for transfers between devices, local(): from_left = lax.ppermute(from_left, 'tensor', upward)  48.7 us
    dot_general x14, matrix products, product(): jnp.einsum(formula, left_side, right_side, preferred_element_type=jnp.flo...  43.7 us
    all_gather x1, waiting for transfers between devices, local(): lax.all_gather(grad_resid.astype(jnp.bfloat16), 'tensor', axis=0, tiled=T...  39.9 us
    dot_general x7, matrix products, transposed_times(): lax.dot_general(left_side, right_side, (((0,), (0,)), ((), ())), preferre...  38.9 us
    reduce_scatter x1, waiting for transfers between devices, local(): lax.psum_scatter(grad_output.astype(jnp.bfloat16), 'dp', scatter_dimensio...  38.8 us
  transfers between devices with their start and end apart: 22, of which 18 were waited for; matrix products, arithmetic and copies ran while one was open for 21% of the time, Pallas kernels for 0%

profile of v1, /device:TPU:0, one launch (start us, length us, event | category | flops | bytes accessed | tf_op | source)
XLA Modules:
  0.0 1044.5 jit_solution(8968679450042554459)
XLA Ops:
  12.6 16.0 %all-reduce.6 = (bf16[1536]{0:T(1024)(128)(2,1)S(1)}, bf16[1536]{0:T(1024)(128)(2,1)}) all-reduce(bf16[1536]{0:T(1024)(128)(2,1)S(1)} %dynamic-update-slice, bf16[1536]{0:T(1024)(128)(2,1)S(1)} %dynamic-update-slice.1), channel_id=1, replica_groups=mesh['dp'=8,'tensor'=4] {'dp'}, use_global_device_ids=true, to_apply=%add | all-reduce | flops 3072 | bytes 12288
  33.7 10.5 %all_gather.48 = bf16[1536,192]{1,0:T(8,128)(2,1)} all-gather(bf16[192,192]{1,0:T(8,128)(2,1)S(1)} %copy-done.26), channel_id=1, replica_groups=mesh['dp'=8,'tensor'=4] {'dp'}, dimensions={0}, use_global_device_ids=true | all-gather | bytes 663552 | tf_op jit(solution)/shard_map/all_gather | solution.py:186
  44.3 11.2 %all_gather.49 = bf16[1536,192]{1,0:T(8,128)(2,1)} all-gather(bf16[192,192]{1,0:T(8,128)(2,1)S(1)} %copy-done.27), channel_id=1, replica_groups=mesh['dp'=8,'tensor'=4] {'dp'}, dimensions={0}, use_global_device_ids=true | all-gather | bytes 663552 | tf_op jit(solution)/shard_map/all_gather | solution.py:187
  56.3 37.9 %all-gather.9.cloned.1.call-done = bf16[1024,1536]{1,0:T(8,128)(2,1)} async-done(((bf16[256,1536]{1,0:T(8,128)(2,1)}), bf16[1024,1536]{1,0:T(8,128)(2,1)}) %all-gather.9.cloned.1.call-update) | async-done | bytes 3145744 | tf_op jit(solution)/shard_map/all_gather | solution.py:208
  98.4 20.2 %all-gather.11.cloned.1.call-done = bf16[1536,384]{1,0:T(8,128)(2,1)} async-done(((bf16[192,384]{1,0:T(8,128)(2,1)}), bf16[1536,384]{1,0:T(8,128)(2,1)}) %all-gather.11.cloned.1.call-update) | async-done | bytes 1179664 | tf_op jit(solution)/shard_map/all_gather | solution.py:185
  130.9 22.1 %while.27 = (s32[]{:T(128)}, bf16[2,512,2,2,96]{1,4,3,2,0:T(8,128)(2,1)}, f32[2,2,2,512]{3,2,1,0:T(2,128)}, s32[2,512]{1,0:T(2,128)}, s32[1024]{0:T(1024)S(1)}, ...) while((s32[]{:T(128)}, ...), condition=%wide.region_7.8_spmd, body=%wide.region_4.7_spmd.sunk | while | flops 830142464 | bytes 28917884 | solution.py:111
  161.9 110.3 %reduce-scatter.12.cloned.1.call-done = f32[256,1536]{1,0:T(8,128)} async-done(((f32[1024,1536]{1,0:T(8,128)}), f32[256,1536]{1,0:T(8,128)}) %reduce-scatter.12.cloned.1.call-update) | async-done | bytes 1572880 | tf_op jit(solution)/shard_map/reduce_scatter | solution.py:231
  284.7 18.6 %collective-permute-done = bf16[256,1536]{1,0:T(8,128)(2,1)S(1)} collective-permute-done((bf16[256,1536]{1,0:T(8,128)(2,1)}, bf16[256,1536]{1,0:T(8,128)(2,1)S(1)}, u32[]{:S(2)}, u32[]{:S(2)}) %collective-permute-start) | collective-permute-done | bytes 786464 | tf_op jit(solution)/shard_map/ppermute | solution.py:285
  303.3 15.1 %collective-permute-start.2 = (bf16[256,1536]{1,0:T(8,128)(2,1)S(1)}, bf16[256,1536]{1,0:T(8,128)(2,1)S(1)}, u32[]{:S(2)}, u32[]{:S(2)}) collective-permute-start(bf16[256,1536]{1,0:T(8,128)(2,1)S(1)} %collective-permute-done), channel_id=1, source_target_pairs={{0,1},{1,2},{2,3},{3,0},{4,5},{5,6},{6,7},{7,4},{8,9},{9,10},{10,1... | collective-permute-start | bytes 2359304 | tf_op jit(solution)/shard_map/ppermute | solution.py:285
  321.6 30.0 %collective-permute-done.2 = bf16[256,1536]{1,0:T(8,128)(2,1)S(1)} collective-permute-done((bf16[256,1536]{1,0:T(8,128)(2,1)S(1)}, bf16[256,1536]{1,0:T(8,128)(2,1)S(1)}, u32[]{:S(2)}, u32[]{:S(2)}) %collective-permute-start.2) | collective-permute-done | bytes 786464 | tf_op jit(solution)/shard_map/ppermute | solution.py:285
  352.6 34.5 %all-gather.15.cloned.1.call-done = bf16[1024,1536]{1,0:T(8,128)(2,1)} async-done(((bf16[256,1536]{1,0:T(8,128)(2,1)}), bf16[1024,1536]{1,0:T(8,128)(2,1)}) %all-gather.15.cloned.1.call-update) | async-done | bytes 3145744 | tf_op jit(solution)/shard_map/all_gather | solution.py:235
  387.1 8.2 fusion.80
  395.3 25.1 %all-gather.17.cloned.1.call-done = bf16[1536,1024]{1,0:T(8,128)(2,1)} async-done(((bf16[192,1024]{1,0:T(8,128)(2,1)}), bf16[1536,1024]{1,0:T(8,128)(2,1)}) %all-gather.17.cloned.1.call-update) | async-done | bytes 3145744 | tf_op jit(solution)/shard_map/all_gather | solution.py:189
  420.4 8.3 fusion.79
  428.7 25.8 %all-gather.21.cloned.1.call-done = bf16[1024,1536]{0,1:T(8,128)(2,1)} async-done(((bf16[1024,192]{0,1:T(8,128)(2,1)}), bf16[1024,1536]{0,1:T(8,128)(2,1)}) %all-gather.21.cloned.1.call-update) | async-done | bytes 3145744 | tf_op jit(solution)/shard_map/all_gather | solution.py:191
  454.5 11.5 %multiply_convert_fusion = (bf16[1024,1024]{1,0:T(8,128)(2,1)S(1)}, bf16[1024,1024]{1,0:T(8,128)(2,1)S(1)}, bf16[1024,1024]{1,0:T(8,128)(2,1)}) fusion(f32[1024,1024]{1,0:T(8,128)} %fusion.79, f32[1024,1024]{1,0:T(8,128)} %fusion.80, bf16[1024,1536]{1,0:T(8,128)(2,1)} %constant_dynamic-update-slice_fusion, bf16[1024,1536]{0,1:T(8,128)(2,1)} %all-gather.21.cloned.1.call-done), kind=kOutput, calls=%fused_computation.68 | convolution fusion | flops 3236954112 | bytes 20971520 | tf_op jit(solution)/shard_map/dot_general | solution.py:23
  474.7 60.5 %reduce-scatter.16.cloned.1.call-done = bf16[256,1536]{1,0:T(8,128)(2,1)} async-done(((bf16[1024,1536]{1,0:T(8,128)(2,1)}), bf16[256,1536]{1,0:T(8,128)(2,1)}) %reduce-scatter.16.cloned.1.call-update) | async-done | bytes 786448 | tf_op jit(solution)/shard_map/reduce_scatter | solution.py:301
  548.3 8.0 convolution_convert_fusion.1
  564.1 39.9 %all-gather.23.cloned.1.call-done = bf16[1024,1536]{1,0:T(8,128)(2,1)} async-done(((bf16[256,1536]{1,0:T(8,128)(2,1)}), bf16[1024,1536]{1,0:T(8,128)(2,1)}) %all-gather.23.cloned.1.call-update) | async-done | bytes 3145744 | tf_op jit(solution)/shard_map/all_gather | solution.py:312
  615.7 68.3 %while.28 = (s32[]{:T(128)}, f32[1024,2,96]{0,2,1:T(8,128)}, f32[1024,2,96]{0,2,1:T(8,128)}, f32[2,512,2,2,96]{1,0,4,3,2:T(2,128)}, bf16[2,512,2,2,96]{1,4,3,2,0...) while((s32[]{:T(128)}, f32[1024,2,96]{0,2,1:T(8,128)}, ...), condition=%wide.region_15.16_spmd.clone, body=%wide.region_13.15_spmd.clone.sunk | while | flops 2039478272 | bytes 50004156 | solution.py:150
  634.1 15.0 %dynamic_update_slice.40 = f32[2,512,2,2,96]{1,0,4,3,2:T(2,128)} dynamic-update-slice(f32[2,512,2,2,96]{1,0,4,3,2:T(2,128)} %get-tuple-element.537, f32[1,512,2,2,96]{1,0,4,3,2:T(1,128)S(1)} %copy.60, s32[]{:T(128)S(6)} %copy.83, s32[]{:T(128)} %constant.90.clone.1..sunk, s32[]{:T(128)} %constant.90.clone.1..sunk, s32[]{:T(128)} %constant.90.clone.1..sunk, s32[]{:T(128)} %constant.90.clone.1..sunk) | dynamic-update-slice | bytes 1572868 | tf_op jit(solution)/shard_map/while/body/jit(dynamic_update_index_in_dim)/dynamic_update_slice | solution.py:150
  669.0 15.0 %dynamic_update_slice.40 = f32[2,512,2,2,96]{1,0,4,3,2:T(2,128)} dynamic-update-slice(f32[2,512,2,2,96]{1,0,4,3,2:T(2,128)} %get-tuple-element.537, f32[1,512,2,2,96]{1,0,4,3,2:T(1,128)S(1)} %copy.60, s32[]{:T(128)S(6)} %copy.83, s32[]{:T(128)} %constant.90.clone.1..sunk, s32[]{:T(128)} %constant.90.clone.1..sunk, s32[]{:T(128)} %constant.90.clone.1..sunk, s32[]{:T(128)} %constant.90.clone.1..sunk) | dynamic-update-slice | bytes 1572868 | tf_op jit(solution)/shard_map/while/body/jit(dynamic_update_index_in_dim)/dynamic_update_slice | solution.py:150
  715.1 8.0 convolution_convert_fusion.3
  727.9 23.2 %reduce-scatter.28.cloned.1.call-done = bf16[192,1024]{1,0:T(8,128)(2,1)} async-done(((bf16[1536,1024]{1,0:T(8,128)(2,1)}), bf16[192,1024]{1,0:T(8,128)(2,1)}) %reduce-scatter.28.cloned.1.call-update) | async-done | bytes 393232 | tf_op jit(solution)/shard_map/reduce_scatter | solution.py:359
  753.0 36.0 %reduce-scatter.24.cloned.1.call-done = bf16[192,192]{1,0:T(8,128)(2,1)} async-done(((bf16[1536,192]{1,0:T(8,128)(2,1)}), bf16[192,192]{1,0:T(8,128)(2,1)}) %reduce-scatter.24.cloned.1.call-update) | async-done | bytes 73744 | tf_op jit(solution)/shard_map/reduce_scatter | solution.py:353
  790.6 36.4 %reduce-scatter.22.cloned.1.call-done = bf16[192,192]{1,0:T(8,128)(2,1)} async-done(((bf16[1536,192]{1,0:T(8,128)(2,1)}), bf16[192,192]{1,0:T(8,128)(2,1)}) %reduce-scatter.22.cloned.1.call-update) | async-done | bytes 73744 | tf_op jit(solution)/shard_map/reduce_scatter | solution.py:350
  828.6 38.8 %reduce-scatter.26.cloned.1.call-done = bf16[384,192]{0,1:T(8,128)(2,1)} async-done(((bf16[384,1536]{0,1:T(8,128)(2,1)}), bf16[384,192]{0,1:T(8,128)(2,1)}) %reduce-scatter.26.cloned.1.call-update) | async-done | bytes 147472 | tf_op jit(solution)/shard_map/reduce_scatter | solution.py:356
  869.0 38.7 %reduce-scatter.20.cloned.1.call-done = bf16[192,384]{1,0:T(8,128)(2,1)} async-done(((bf16[1536,384]{1,0:T(8,128)(2,1)}), bf16[192,384]{1,0:T(8,128)(2,1)}) %reduce-scatter.20.cloned.1.call-update) | async-done | bytes 147472 | tf_op jit(solution)/shard_map/reduce_scatter | solution.py:347
  909.4 60.9 %reduce-scatter.18.cloned.1.call-done = bf16[256,1536]{1,0:T(8,128)(2,1)} async-done(((bf16[1024,1536]{1,0:T(8,128)(2,1)}), bf16[256,1536]{1,0:T(8,128)(2,1)}) %reduce-scatter.18.cloned.1.call-update) | async-done | bytes 786448 | tf_op jit(solution)/shard_map/reduce_scatter | solution.py:334
  972.0 13.5 %all-reduce.5 = (bf16[1536]{0:T(1024)(128)(2,1)S(1)}, bf16[1536]{0:T(1024)(128)(2,1)S(1)}) all-reduce(bf16[1536]{0:T(1024)(128)(2,1)S(1)} %get-tuple-element.256, bf16[1536]{0:T(1024)(128)(2,1)S(1)} %copy-done.32), channel_id=13, replica_groups=mesh['dp'=8,'tensor'=4] {'dp'}, use_global_device_ids=true, to_apply=%region_26.27.clone | all-reduce | flops 3072 | bytes 12288
  985.7 12.1 %all-reduce.4 = (f32[192]{0:T(256)}, f32[192]{0:T(256)}) all-reduce(f32[192]{0:T(256)S(1)} %get-tuple-element.338, f32[192]{0:T(256)S(1)} %get-tuple-element.337), channel_id=1, replica_groups=mesh['dp'=8,'tensor'=4] {'tensor'}, use_global_device_ids=true, to_apply=%region_27.28 | all-reduce | flops 384 | bytes 3072 | tf_op jit(solution)/shard_map/psum | solution.py:376
  997.7 35.5 %reduce-scatter.14.cloned.1.call-done = bf16[256,1536]{1,0:T(8,128)(2,1)} async-done(((bf16[1024,1536]{1,0:T(8,128)(2,1)}), bf16[256,1536]{1,0:T(8,128)(2,1)}) %reduce-scatter.14.cloned.1.call-update) | async-done | bytes 786448 | tf_op jit(solution)/shard_map/reduce_scatter | solution.py:248
  (238 shorter events, 203.2 us)
Async XLA Ops:
  7.2 86.9 %all-gather.9.cloned.1.call-start = ((), (), s32[]{:S(2)}) async-start(), calls=%async_computation.11 | async-start | bytes 3932160 | tf_op jit(solution)/shard_map/all_gather | solution.py:208
  31.2 87.4 %all-gather.11.cloned.1.call-start = ((), (), s32[]{:S(2)}) async-start(), calls=%async_computation.12 | async-start | bytes 1327104 | tf_op jit(solution)/shard_map/all_gather | solution.py:185
  31.9 123.2 %all-gather.13.cloned.1.call-start = ((), (), s32[]{:S(2)}) async-start(), calls=%async_computation.13 | async-start | bytes 1327104 | tf_op jit(solution)/shard_map/all_gather | solution.py:188
  32.7 239.5 %reduce-scatter.12.cloned.1.call-start = ((), (), s32[]{:S(2)}) async-start(), calls=%async_computation.14 | async-start | bytes 7864320 | tf_op jit(solution)/shard_map/reduce_scatter | solution.py:231
  56.2 65.1 %copy-start.10 = (f32[1024,48]{0,1:T(8,128)}, f32[1024,48]{0,1:T(8,128)S(1)}, u32[]{:S(2)}) copy-start(f32[1024,48]{0,1:T(8,128)S(1)} %get-tuple-element.333) | copy-start | bytes 589828
  56.3 65.1 %copy-start.12 = (f32[1024,48]{0,1:T(8,128)}, f32[1024,48]{0,1:T(8,128)S(1)}, u32[]{:S(2)}) copy-start(f32[1024,48]{0,1:T(8,128)S(1)} %get-tuple-element.334) | copy-start | bytes 589828
  161.2 111.0 %copy-start = (f32[256,1536]{1,0:T(8,128)S(1)}, f32[256,1536]{1,0:T(8,128)}, u32[]{:S(2)}) copy-start(f32[256,1536]{1,0:T(8,128)} %param.16) | copy-start | bytes 4718596
  161.3 191.3 %all-gather.19.cloned.1.call-start = ((), (), s32[]{:S(2)}) async-start(), calls=%async_computation.17 | async-start | bytes 3538944 | tf_op jit(solution)/shard_map/all_gather | solution.py:190
  161.9 225.2 %all-gather.15.cloned.1.call-start = ((), (), s32[]{:S(2)}) async-start(), calls=%async_computation.15 | async-start | bytes 3932160 | tf_op jit(solution)/shard_map/all_gather | solution.py:235
  276.1 144.3 %all-gather.17.cloned.1.call-start = ((), (), s32[]{:S(2)}) async-start(), calls=%async_computation.16 | async-start | bytes 3538944 | tf_op jit(solution)/shard_map/all_gather | solution.py:189
  276.9 177.6 %all-gather.21.cloned.1.call-start = ((), (), s32[]{:S(2)}) async-start(), calls=%async_computation.18 | async-start | bytes 3538944 | tf_op jit(solution)/shard_map/all_gather | solution.py:191
  277.6 257.6 %reduce-scatter.16.cloned.1.call-start = ((), (), s32[]{:S(2)}) async-start(), calls=%async_computation.20 | async-start | bytes 3932160 | tf_op jit(solution)/shard_map/reduce_scatter | solution.py:301
  280.8 22.5 %collective-permute-start = (bf16[256,1536]{1,0:T(8,128)(2,1)}, bf16[256,1536]{1,0:T(8,128)(2,1)S(1)}, u32[]{:S(2)}, u32[]{:S(2)}) collective-permute-start(bf16[256,1536]{1,0:T(8,128)(2,1)} %get-tuple-element.311), channel_id=1, source_target_pairs={{0,1},{1,2},{2,3},{3,0},{4,5},{5,6},{6,7},{7,4},{8,9},{9,10},{10,1... | collective-permute-start | bytes 2359304 | tf_op jit(solution)/shard_map/ppermute | solution.py:285
  282.3 37.3 %collective-permute-start.1 = (bf16[256,1536]{1,0:T(8,128)(2,1)}, bf16[256,1536]{1,0:T(8,128)(2,1)}, u32[]{:S(2)}, u32[]{:S(2)}) collective-permute-start(bf16[256,1536]{1,0:T(8,128)(2,1)} %get-tuple-element.311), channel_id=1, source_target_pairs={{0,3},{1,0},{2,1},{3,2},{4,7},{5,4},{6,5},{7,6},{8,11},{9,8},{10,9... | collective-permute-start | bytes 2359304 | tf_op jit(solution)/shard_map/ppermute | solution.py:288
  303.3 48.4 %collective-permute-start.2 = (bf16[256,1536]{1,0:T(8,128)(2,1)S(1)}, bf16[256,1536]{1,0:T(8,128)(2,1)S(1)}, u32[]{:S(2)}, u32[]{:S(2)}) collective-permute-start(bf16[256,1536]{1,0:T(8,128)(2,1)S(1)} %collective-permute-done), channel_id=1, source_target_pairs={{0,1},{1,2},{2,3},{3,0},{4,5},{5,6},{6,7},{7,4},{8,9},{9,10},{10,1... | collective-permute-start | bytes 2359304 | tf_op jit(solution)/shard_map/ppermute | solution.py:285
  474.6 60.6 %copy-start.3 = (f32[256,1536]{1,0:T(8,128)S(1)}, f32[256,1536]{1,0:T(8,128)}, u32[]{:S(2)}) copy-start(f32[256,1536]{1,0:T(8,128)} %copy-done.2) | copy-start | bytes 4718596
  474.6 129.4 %all-gather.23.cloned.1.call-start = ((), (), s32[]{:S(2)}) async-start(), calls=%async_computation.21 | async-start | bytes 3932160 | tf_op jit(solution)/shard_map/all_gather | solution.py:312
  540.6 183.2 %reduce-scatter.32.cloned.1.call-start = ((), (), s32[]{:S(2)}) async-start(), calls=%async_computation.29 | async-start | bytes 3538944 | tf_op jit(solution)/shard_map/reduce_scatter | solution.py:365
  548.3 177.5 %reduce-scatter.30.cloned.1.call-start = ((), (), s32[]{:S(2)}) async-start(), calls=%async_computation.28 | async-start | bytes 3538944 | tf_op jit(solution)/shard_map/reduce_scatter | solution.py:362
  556.3 194.7 %reduce-scatter.28.cloned.1.call-start = ((), (), s32[]{:S(2)}) async-start(), calls=%async_computation.27 | async-start | bytes 3538944 | tf_op jit(solution)/shard_map/reduce_scatter | solution.py:359
  564.1 224.9 %reduce-scatter.24.cloned.1.call-start = ((), (), s32[]{:S(2)}) async-start(), calls=%async_computation.25 | async-start | bytes 884736 | tf_op jit(solution)/shard_map/reduce_scatter | solution.py:353
  689.9 137.1 %reduce-scatter.22.cloned.1.call-start = ((), (), s32[]{:S(2)}) async-start(), calls=%async_computation.24 | async-start | bytes 884736 | tf_op jit(solution)/shard_map/reduce_scatter | solution.py:350
  696.5 170.8 %reduce-scatter.26.cloned.1.call-start = ((), (), s32[]{:S(2)}) async-start(), calls=%async_computation.26 | async-start | bytes 1327104 | tf_op jit(solution)/shard_map/reduce_scatter | solution.py:356
  701.4 206.4 %reduce-scatter.20.cloned.1.call-start = ((), (), s32[]{:S(2)}) async-start(), calls=%async_computation.23 | async-start | bytes 1327104 | tf_op jit(solution)/shard_map/reduce_scatter | solution.py:347
  708.8 261.5 %reduce-scatter.18.cloned.1.call-start = ((), (), s32[]{:S(2)}) async-start(), calls=%async_computation.22 | async-start | bytes 3932160 | tf_op jit(solution)/shard_map/reduce_scatter | solution.py:334
  714.9 318.4 %reduce-scatter.14.cloned.1.call-start = ((), (), s32[]{:S(2)}) async-start(), calls=%async_computation.19 | async-start | bytes 3932160 | tf_op jit(solution)/shard_map/reduce_scatter | solution.py:248
  723.1 247.2 %copy-start.1 = (f32[256,1536]{1,0:T(8,128)S(1)}, f32[256,1536]{1,0:T(8,128)}, u32[]{:S(2)}) copy-start(f32[256,1536]{1,0:T(8,128)} %param.16) | copy-start | bytes 4718596
  723.1 247.2 %copy-start.25 = (f32[1536]{0:T(1024)S(1)}, f32[1536]{0:T(1024)}, u32[]{:S(2)}) copy-start(f32[1536]{0:T(1024)} %copy-done.24) | copy-start | bytes 18436
  723.1 247.2 %copy-start.31 = (f32[256]{0:T(256)S(1)}, f32[256]{0:T(256)}, u32[]{:S(2)}) copy-start(f32[256]{0:T(256)} %copy-done.30) | copy-start | bytes 3076
  725.8 246.3 %copy-start.32 = (bf16[1536]{0:T(1024)(128)(2,1)S(1)}, bf16[1536]{0:T(1024)(128)(2,1)}, u32[]{:S(2)}) copy-start(bf16[1536]{0:T(1024)(128)(2,1)} %get-tuple-element.254) | copy-start | bytes 9220
  725.8 307.5 %copy-start.29 = (f32[256]{0:T(256)S(1)}, f32[256]{0:T(256)}, u32[]{:S(2)}) copy-start(f32[256]{0:T(256)} %copy-done.28) | copy-start | bytes 3076
  725.8 307.5 %copy-start.34 = (f32[256]{0:T(256)S(1)}, f32[256]{0:T(256)}, u32[]{:S(2)}) copy-start(f32[256]{0:T(256)} %copy-done.33) | copy-start | bytes 3076
  (31 other events, 277.4 us)
Sparse Core Ops, SparseCore 0:
  31.3 62.7 all-gather.8
  96.0 22.5 all-gather.10
  120.5 23.9 all-gather.12
  161.4 110.7 reduce-scatter.11
  273.9 32.6 all-gather.18
  308.7 78.3 all-gather.14
  388.9 31.4 all-gather.16
  422.3 32.1 all-gather.20
  474.8 60.3 reduce-scatter.15
  540.7 63.3 all-gather.22
  607.4 44.6 reduce-scatter.31
  655.4 46.0 reduce-scatter.29
  704.9 46.0 reduce-scatter.27
  754.0 34.9 reduce-scatter.23
  792.0 34.9 reduce-scatter.21
  830.6 36.6 reduce-scatter.25
  871.0 36.6 reduce-scatter.19
  909.9 60.3 reduce-scatter.17
  972.6 60.5 reduce-scatter.13
